TPU v7x, 32 devices: a whole 2x2x4 slice. The times are simulated.
32 devices in a mesh: groups: 2 (over y), ctx: 4 (over z), head: 2 (over x), qsub: 2 (over core).
Axes of the slice: x: 2, y: 2, z: 4, core: 2. Of those that a mesh axis runs over, the one named last changes fastest.
Arguments:
- queries: bfloat16 [4096, 2, 8, 128], P(('groups', 'ctx'), 'head', 'qsub'), parts along dimension 0, may hold values from -7 to 7
- key_states: bfloat16 [4096, 2, 128], P(('groups', 'ctx'), 'head'), parts along dimension 0, may hold values from -4 to 4
- value_states: bfloat16 [4096, 2, 128], P(('groups', 'ctx'), 'head'), parts along dimension 0, may hold values from -6 to 6
- block_table: int32 [16, 7], P(('groups', 'ctx')), parts along dimension 0, may hold values from -1 to 6, as said below
Outputs:
- attended: bfloat16 [4096, 2, 8, 128], P(('groups', 'ctx'), 'head', 'qsub'), parts along dimension 0
There are 2 independent parts, one for each index of `groups`. A program takes and returns all parts, laid end to end along the dimension named above; each array names one. Nothing has to cross between parts.
Inputs may be any that keep to these rules, and one draw needn't show every extreme that they name: `block_table`: entry [b, k] is -1 or b - 2 ** k, and never below 0; it is b - 2 ** k wherever that value is 0 or 1, and in column 0 wherever b >= 1.
All inputs are finite; a program needn't handle non-finite values.
Results may differ from a plain program's by a relative error of at most 0.0044.
Values may be sent and summed in bfloat16 or wider, within the bound.
No kernel may reach another device: no remote copies, remote signals or barrier semaphores. Data moves between devices by JAX's collectives and lax.ppermute only.
A program may use at most 64 MiB of HBM per device.

v0:
```python
import functools
import math
from functools import reduce

import jax
import jax.numpy as jnp
from jax import lax
from jax.experimental import pallas as pl
from jax.experimental.pallas import tpu as pltpu
from jax.sharding import PartitionSpec as P


DH = 128
BLOCK = 256
SINKS = 4
LEVELS = 7
TILE = 512
NEG = -1e30
BIG = 1e30
EXP2_SCALE = DH ** (-0.5) * math.log2(math.e)
ONES = 16


def named(table_ref, i, u):
    return reduce(lambda a, b: a | b, [table_ref[i, level] == u for level in range(LEVELS)])


def counts_of(kind, table_ref, i, block, u, first_here, blocks_here):
    before = (u >= 0) & (u < block)
    elsewhere = (u < first_here) | (u >= first_here + blocks_here)
    if kind == "all":
        return before & elsewhere & ((u < SINKS) | named(table_ref, i, u))
    if kind == "sink":
        return before & elsewhere & (u < SINKS)
    return before & elsewhere & (u >= SINKS) & named(table_ref, i, u)


def split_queries(q):
    scaled = q.astype(jnp.float32) * EXP2_SCALE
    high = scaled.astype(jnp.bfloat16)
    low = (scaled - high.astype(jnp.float32)).astype(jnp.bfloat16)
    return jnp.concatenate([high, low], axis=1)


def scores(k, q):
    return lax.dot_general(k, q, (((1,), (1,)), ((), ())), preferred_element_type=jnp.float32)


def top_of(s):
    return jnp.max(s, axis=0, keepdims=True)


def weights(s, shift):
    return jnp.exp2(s - shift).astype(jnp.bfloat16)


def keep_state(acc_ref, stat_ref, cols, acc, highest, total):
    acc_ref[:, cols] = acc
    stat_ref[:8, cols] = jnp.broadcast_to(highest, total.shape)
    stat_ref[8:, cols] = total


def local_stage(i, per_head, cores, q_ref, *refs):
    refs = list(refs)
    parts = [refs.pop(0) for _ in range(cores)]
    table_ref = refs.pop(0) if len(refs) == 7 else None
    acc_ref, stat_ref, split_ref, k_ref, v_ref, vt_ref = refs
    core = lax.axis_index("qsub")
    part = parts[0].shape[1]
    for shift, ref in enumerate(parts):
        at = pl.ds(pl.multiple_of(lax.rem(core - shift + cores, cores) * part, part), part)
        k_ref[at, :DH] = ref[0]
        k_ref[at, DH:] = ref[0]
        v_ref[at, :] = ref[1]
    keys = (i + 1) * BLOCK
    vt_ref[:DH, :] = v_ref[:keys, :].T
    vt_ref[DH:, :] = jnp.ones((ONES, keys), vt_ref.dtype)
    rows_per_block = BLOCK * per_head
    tokens = TILE // per_head
    first_here = lax.axis_index("ctx") * (k_ref.shape[0] // BLOCK)
    for t in range(rows_per_block // TILE):
        q = split_queries(q_ref[pl.ds(i * rows_per_block + t * TILE, TILE), :])
        split_ref[pl.ds(t * TILE, TILE), :] = q
        edge = i * BLOCK + t * tokens
        items = []
        for j in range(i):
            s = scores(k_ref[pl.ds(j * BLOCK, BLOCK), :], q)
            if j < i - 1:
                u = first_here + j
                s = jnp.where((u < SINKS) | named(table_ref, i, u), s, NEG)
            items.append(s)
        if t:
            items.append(scores(k_ref[pl.ds(i * BLOCK, t * tokens), :], q))
        token = lax.broadcasted_iota(jnp.int32, (tokens, TILE), 1) // per_head
        mask = lax.broadcasted_iota(jnp.int32, (tokens, TILE), 0) <= token
        items.append(jnp.where(mask, scores(k_ref[pl.ds(edge, tokens), :], q), NEG))
        highest = reduce(jnp.maximum, [top_of(s) for s in items])
        w = jnp.concatenate([weights(s, highest) for s in items], axis=0)
        sums = jnp.dot(vt_ref[:, : edge + tokens], w, preferred_element_type=jnp.float32)
        keep_state(acc_ref, stat_ref, pl.ds(t * TILE, TILE), sums[:DH], highest, sums[DH : DH + 8])


def flags_stage(stages, blocks_here, table_ref, flags_ref):
    me, core = lax.axis_index("ctx"), lax.axis_index("qsub")
    first_here = me * blocks_here
    at = 0
    for pieces in stages:
        for kind, base, count in pieces:
            start = base(me, core)
            for j in range(count):
                u = jnp.where(start < 0, -1, start + j)
                for i in range(blocks_here):
                    counts = counts_of(kind, table_ref, i, first_here + i, u, first_here, blocks_here)
                    flags_ref[at : at + 1, :] = jnp.full((1, TILE), jnp.where(counts, 0.0, BIG), jnp.float32)
                    at += 1


def arrival_stage(source, row_of, operands, blocks_here, last, *refs):
    refs = list(refs)
    flags_ref = None if row_of is None else refs.pop(0)
    state_in = [(refs.pop(0), refs.pop(0), refs.pop(0)) for _ in range(blocks_here)]
    arrived = [refs.pop(0) for _ in range(operands)]
    if last:
        out_hbm, out_ref, k_ref, vt_ref, sems = refs
    else:
        state_out = [(refs.pop(0), refs.pop(0)) for _ in range(blocks_here)]
        k_ref, vt_ref = refs
    me = lax.axis_index("ctx")
    origin = source(me)
    some = (origin >= 0) & (origin < me)
    key_blocks = k_ref.shape[0] // BLOCK
    rows_per_block = state_in[0][0].shape[1]
    tile = min(TILE, k_ref.shape[0])
    depth = 2 * TILE // tile
    per_block = rows_per_block // tile
    tiles = per_block * blocks_here

    def place(t):
        return t // per_block, pl.ds(t % per_block * tile, tile)

    def finish(t, acc, highest, total):
        i, cols = place(t)
        if not last:
            keep_state(*state_out[i], cols, acc, highest, total)
            return
        rows = pl.ds(t * tile, tile)
        out_ref[rows, :] = (acc * (1.0 / total[:1])).astype(out_ref.dtype).T
        pltpu.make_async_copy(out_ref.at[rows], out_hbm.at[rows], sems.at[t]).start()

    @pl.when(some)
    def _():
        at = 0
        for ref in arrived:
            span = pl.ds(at, ref.shape[1])
            k_ref[span, :DH] = ref[0]
            k_ref[span, DH:] = ref[0]
            vt_ref[:DH, span] = ref[1].T
            at += ref.shape[1]
        vt_ref[DH:, :] = jnp.ones((ONES, at), vt_ref.dtype)
        k, vt = k_ref[...], vt_ref[...]

        def begin(t):
            i, cols = place(t)
            return scores(k, state_in[i][2][cols, :])

        raw = [begin(t) for t in range(min(depth, tiles))]
        for t in range(tiles):
            if t + depth < tiles:
                raw.append(begin(t + depth))
            s = raw.pop(0)
            i, cols = place(t)
            acc_in, stat_in, _ = state_in[i]
            before = stat_in[:1, cols]
            if row_of is None:
                highest = jnp.maximum(before, top_of(s))
                w = weights(s, highest)
            else:
                parts = [s[j * BLOCK : (j + 1) * BLOCK] for j in range(key_blocks)]
                at = [row_of + j * blocks_here + i for j in range(key_blocks)]
                off = [flags_ref[n : n + 1, :tile] for n in at]
                highest = reduce(jnp.maximum, [top_of(part) - o for part, o in zip(parts, off)], before)
                w = jnp.concatenate([weights(part, highest + o) for part, o in zip(parts, off)], axis=0)
            sums = jnp.dot(vt, w, preferred_element_type=jnp.float32)
            keep = jnp.exp2(before - highest)
            finish(t, acc_in[:, cols] * keep + sums[:DH], highest, stat_in[8:, cols] * keep + sums[DH : DH + 8])

    @pl.when(jnp.logical_not(some))
    def _():
        for t in range(tiles):
            i, cols = place(t)
            acc_in, stat_in, _ = state_in[i]
            finish(t, acc_in[:, cols], stat_in[:1, cols], stat_in[8:, cols])

    if last:
        for t in range(tiles):
            rows = pl.ds(t * tile, tile)
            pltpu.make_async_copy(out_ref.at[rows], out_hbm.at[rows], sems.at[t]).wait()


VMEM_SPEC = pl.BlockSpec(memory_space=pltpu.VMEM)
SMEM_SPEC = pl.BlockSpec(memory_space=pltpu.SMEM)
ANY_SPEC = pl.BlockSpec(memory_space=pl.ANY)
PARAMS = pltpu.CompilerParams(vmem_limit_bytes=16 << 20)


def state_shapes(rows):
    return [jax.ShapeDtypeStruct((DH, rows), jnp.float32), jax.ShapeDtypeStruct((16, rows), jnp.float32)]


def cost(rows, keys):
    return pl.CostEstimate(flops=4 * rows * keys * DH, bytes_accessed=8 * rows * DH, transcendentals=rows * keys)


def call_local(i, q, parts, table, per_head):
    tokens = sum(a.shape[1] for a in parts)
    rows = BLOCK * per_head
    needs_table = i > 1
    return pl.pallas_call(
        functools.partial(local_stage, i, per_head, len(parts)),
        in_specs=[VMEM_SPEC] * (1 + len(parts)) + [SMEM_SPEC] * needs_table,
        out_specs=[VMEM_SPEC] * 3,
        out_shape=[*state_shapes(rows), jax.ShapeDtypeStruct((rows, 2 * DH), q.dtype)],
        scratch_shapes=[
            pltpu.VMEM((tokens, 2 * DH), q.dtype),
            pltpu.VMEM((tokens, DH), q.dtype),
            pltpu.VMEM((DH + ONES, (i + 1) * BLOCK), q.dtype),
        ],
        cost_estimate=cost(rows, (i + 1) * BLOCK),
        compiler_params=PARAMS,
    )(*([q, *parts] + [table] * needs_table))


def call_flags(stages, table, blocks_here):
    entries = sum(count for pieces in stages for _, _, count in pieces) * blocks_here
    return pl.pallas_call(
        functools.partial(flags_stage, stages, blocks_here),
        in_specs=[SMEM_SPEC],
        out_specs=VMEM_SPEC,
        out_shape=jax.ShapeDtypeStruct((-(-entries // 8) * 8, TILE), jnp.float32),
        compiler_params=PARAMS,
        name="flags",
    )(table)


def call_arrival(source, row_of, arrays, flags, state, last=False):
    rows_per_block = state[0][0].shape[1]
    rows = rows_per_block * len(state)
    dtype = arrays[0].dtype
    keys = sum(a.shape[1] for a in arrays)
    scratch = [pltpu.VMEM((keys, 2 * DH), dtype), pltpu.VMEM((DH + ONES, keys), dtype)]
    if last:
        scratch = [pltpu.VMEM((rows, DH), dtype), *scratch, pltpu.SemaphoreType.DMA((rows // min(TILE, keys),))]
    args = [] if row_of is None else [flags]
    args += [*[a for block in state for a in block], *arrays]
    out = pl.pallas_call(
        functools.partial(arrival_stage, source, row_of, len(arrays), len(state), last),
        in_specs=[VMEM_SPEC] * len(args),
        out_specs=ANY_SPEC if last else [VMEM_SPEC] * (2 * len(state)),
        out_shape=jax.ShapeDtypeStruct((rows, DH), dtype) if last else state_shapes(rows_per_block) * len(state),
        scratch_shapes=scratch,
        cost_estimate=cost(rows, keys),
        compiler_params=PARAMS,
    )(*args)
    return out if last else [(out[2 * i], out[2 * i + 1], block[2]) for i, block in enumerate(state)]


def shards(queries, key_states, value_states, block_table):
    tokens = queries.shape[0]
    per_head = queries.shape[2]
    blocks_here = tokens // BLOCK
    context_count = lax.axis_size("ctx")
    cores = lax.axis_size("qsub")
    per_core = blocks_here // cores
    core = lax.axis_index("qsub")
    q = queries.reshape(tokens * per_head, DH)
    k = key_states.reshape(tokens, DH)
    v = value_states.reshape(tokens, DH)

    part = per_core * BLOCK
    packed = jnp.stack(
        [lax.dynamic_slice_in_dim(k, core * part, part), lax.dynamic_slice_in_dim(v, core * part, part)]
    )

    def swapped(arrived):
        return [
            lax.ppermute(arrived, "qsub", [(c, (c + shift) % cores) for c in range(cores)])
            for shift in range(1, cores)
        ]

    def hop(block, route):
        return lax.ppermute(block, "ctx", route)

    def local(i, parts):
        return call_local(i, q, parts, block_table, per_head)

    def pieces_of(kind, source):
        pieces = []
        for shift in range(cores):
            base = lambda me, core, shift=shift: jnp.where(
                source(me) < 0, -1, source(me) * blocks_here + lax.rem(core - shift + cores, cores) * per_core
            )
            pieces.append((kind, base, per_core))
        return pieces

    def flags_of(stages):
        return call_flags(stages, block_table, blocks_here)

    if context_count == 4:
        ring = [0, 1, 2, 3]
        after = {d: ring[(ring.index(d) + 1) % 4] for d in ring}
        before = {d: ring[(ring.index(d) - 1) % 4] for d in ring}
        forward = [(d, after[d]) for d in range(4)]
        backward = [(d, before[d]) for d in range(4)]
        origins = [before, after, {0: 3, 1: 2, 2: 0, 3: 1}]
        sources = [
            lambda me, pairs=pairs: reduce(lambda acc, d: jnp.where(me == d, pairs[d], acc), range(4), jnp.int32(0))
            for pairs in origins
        ]
        tabled = [any(o < d and (o + 1) * blocks_here > SINKS for d, o in pairs.items()) for pairs in origins]
        row_of, listed = [], []
        for n in range(3):
            row_of.append(len(listed) * per_core * cores * blocks_here if tabled[n] else None)
            if tabled[n]:
                listed.append(pieces_of("all", sources[n]))

        one = hop(packed, forward)
        parts = [packed, *swapped(packed)]
        state = [local(0, parts)]
        other = hop(packed, backward)
        flags = flags_of(listed) if listed else None
        state += [local(i, parts) for i in range(1, blocks_here)]
        one, state = lax.optimization_barrier((one, state))
        swap = swapped(one)
        route = [(c, (c + 1) % cores) for c in range(cores)]
        route += [(a * cores + c, b * cores + c) for a, b in ((1, 2), (2, 3), (3, 1)) for c in range(cores)]
        two = lax.ppermute(one, ("ctx", "qsub"), route)
        state = call_arrival(sources[0], row_of[0], [one, *swap], flags, state)
        for n, arrived in ((1, other), (2, two)):
            arrived, state = lax.optimization_barrier((arrived, state))
            swap = swapped(arrived)
            row = row_of[n]
            state = call_arrival(sources[n], row, [arrived], flags, state)
            row = None if row is None else row + per_core * blocks_here
            state = call_arrival(sources[n], row, swap, flags, state, last=n == 2)
        attended = state
    else:
        parts = [packed, *swapped(packed)]
        state = [local(i, parts) for i in range(blocks_here)]
        wanted = []
        for level in range(LEVELS):
            amount = max(2**level // blocks_here, 1)
            if amount < context_count and amount not in wanted:
                wanted.append(amount)
        roots = -(-SINKS // blocks_here)
        position = lax.axis_index("ctx")
        shared = [
            lax.psum(jnp.where(position == root, packed, jnp.zeros_like(packed)), "ctx") for root in range(roots)
        ]
        stages = []
        moved, reached = packed, 0
        for amount in wanted:
            step = amount - reached
            moved = hop(moved, [(d, d + step) for d in range(context_count - step)])
            reached = amount
            stages.append((moved, "level", lambda me, amount=amount: jnp.maximum(me - amount, -1)))
        for root, arrived in enumerate(shared):
            stages.append((arrived, "sink", lambda me, root=root: jnp.int32(root)))
        flags = flags_of([pieces_of(kind, source) for _, kind, source in stages])
        for n, (arrived, _, source) in enumerate(stages):
            row = n * per_core * cores * blocks_here
            arrays = [arrived, *swapped(arrived)]
            state = call_arrival(source, row, arrays, flags, state, last=n == len(stages) - 1)
        attended = state
    return attended.reshape(tokens, 1, per_head, DH)


def solution(mesh):
    placed = (
        P(("groups", "ctx"), "head", "qsub", None),
        P(("groups", "ctx"), "head", None),
        P(("groups", "ctx"), "head", None),
        P(("groups", "ctx"), None),
    )

    return jax.shard_map(
        shards,
        mesh=mesh,
        in_specs=placed,
        out_specs=P(("groups", "ctx"), "head", "qsub", None),
        check_vma=False,
    )
```

profile of v0, /device:TPU:9, one launch (start us, length us, event | category | flops | bytes accessed | tf_op | source)
XLA Modules:
  0.0 24.0 jit_solution(15247475455059399908)
XLA Ops:
  0.0 0.9 %dynamic-slice_bitcast_fusion = (bf16[1,256,128]{2,1,0:T(8,128)(2,1)S(1)}, bf16[1,256,128]{2,1,0:T(8,128)(2,1)S(1)}) fusion(bf16[512,1,128]{2,0,1:T(8,128)(2,1)} %param.6, s32[]{:T(128)S(6)} %select_n.4, bf16[512,1,128]{2,0,1:T(8,128)(2,1)} %param.5), kind=kLoop, calls=%fused_computation.1 | loop fusion | bytes 262148 | tf_op jit(solution)/shard_map/stack | solution.py:280
  1.0 0.7 %collective-permute-start.1 = (bf16[2,256,128]{2,1,0:T(8,128)(2,1)S(1)}, bf16[2,256,128]{2,1,0:T(8,128)(2,1)S(1)}, u32[]{:S(2)}, u32[]{:S(2)}) collective-permute-start(bf16[2,256,128]{2,1,0:T(8,128)(2,1)S(1)} %pad_maximum_fusion.refs_0_), channel_id=1, source_target_pairs={{0,1},{1,0},{2,3},{3,2},{4,5},{5,4},{6,7},{7,6},{8,9},{9,8},{10,11... | collective-permute-start | bytes 393224 | tf_op jit(solution)/shard_map/ppermute | solution.py:286
  1.7 1.3 %collective-permute-start = (bf16[2,256,128]{2,1,0:T(8,128)(2,1)S(1)}, bf16[2,256,128]{2,1,0:T(8,128)(2,1)S(1)}, u32[]{:S(2)}, u32[]{:S(2)}) collective-permute-start(bf16[2,256,128]{2,1,0:T(8,128)(2,1)S(1)} %pad_maximum_fusion.refs_0_), channel_id=1, source_target_pairs={{0,4},{4,8},{8,12},{12,0},{1,5},{5,9},{9,13},{13,1},{2,6},{6,10},{... | collective-permute-start | bytes 393224 | tf_op jit(solution)/shard_map/ppermute | solution.py:291
  3.0 0.0 collective-permute-done.1.refs_1_
  3.0 0.0 copy-done
  3.0 0.8 %shard_map.46 = (f32[128,1024]{1,0:T(8,128)S(1)}, f32[16,1024]{1,0:T(8,128)S(1)}, bf16[1024,256]{1,0:T(8,128)(2,1)S(1)}) custom-call(bf16[2048,128]{1,0:T(8,128)(2,1)S(1)} %bitcast.8, bf16[2,256,128]{2,1,0:T(8,128)(2,1)S(1)} %pad_maximum_fusion.refs_0_, bf16[2,256,128]{2,1,0:T(8,128)(2,1)S(1)} %collective-permute-done.1.refs_1_), custom_call_target="tpu_custom_call" | custom-call | flops 134217728 | bytes 1048576 | tf_op jit(solution)/shard_map/pallas_call | solution.py:218
  3.9 1.2 %shard_map.47 = (f32[128,1024]{1,0:T(8,128)S(1)}, f32[16,1024]{1,0:T(8,128)S(1)}, bf16[1024,256]{1,0:T(8,128)(2,1)S(1)}) custom-call(bf16[2048,128]{1,0:T(8,128)(2,1)S(1)} %bitcast.9, bf16[2,256,128]{2,1,0:T(8,128)(2,1)S(1)} %pad_maximum_fusion.refs_0_, bf16[2,256,128]{2,1,0:T(8,128)(2,1)S(1)} %collective-permute-done.1.refs_1_), custom_call_target="tpu_custom_call" | custom-call | flops 268435456 | bytes 1048576 | tf_op jit(solution)/shard_map/pallas_call | solution.py:218
  5.0 1.7 %collective-permute-done.refs_7_ = bf16[2,256,128]{2,1,0:T(8,128)(2,1)S(1)} collective-permute-done((bf16[2,256,128]{2,1,0:T(8,128)(2,1)S(1)}, bf16[2,256,128]{2,1,0:T(8,128)(2,1)S(1)}, u32[]{:S(2)}, u32[]{:S(2)}) %collective-permute-start) | collective-permute-done | bytes 131104 | tf_op jit(solution)/shard_map/ppermute | solution.py:291
  6.7 0.9 %collective-permute-start.4 = (bf16[2,256,128]{2,1,0:T(8,128)(2,1)S(1)}, bf16[2,256,128]{2,1,0:T(8,128)(2,1)S(1)}, u32[]{:S(2)}, u32[]{:S(2)}) collective-permute-start(bf16[2,256,128]{2,1,0:T(8,128)(2,1)S(1)} %collective-permute-done.refs_7_), channel_id=1, source_target_pairs={{0,1},{1,0},{2,3},{3,2},{4,5},{5,4},{6,7},{7,6},{8,9},{9,8},{10,11... | collective-permute-start | bytes 393224 | tf_op jit(solution)/shard_map/ppermute | solution.py:286
  7.6 2.0 %collective-permute-start.3 = (bf16[2,256,128]{2,1,0:T(8,128)(2,1)S(1)}, bf16[2,256,128]{2,1,0:T(8,128)(2,1)S(1)}, u32[]{:S(2)}, u32[]{:S(2)}) collective-permute-start(bf16[2,256,128]{2,1,0:T(8,128)(2,1)S(1)} %pad_maximum_fusion.refs_0_), channel_id=1, source_target_pairs={{0,12},{4,0},{8,4},{12,8},{1,13},{5,1},{9,5},{13,9},{2,14},{6,2},{... | collective-permute-start | bytes 393224 | tf_op jit(solution)/shard_map/ppermute | solution.py:291
  9.7 0.6 %flags.1.refs_0_ = f32[8,512]{1,0:T(8,128)S(1)} custom-call(s32[2,7]{1,0:T(2,128)S(1)} %copy-done.1), custom_call_target="tpu_custom_call" | custom-call | tf_op jit(solution)/shard_map/flags/pallas_call | solution.py:235
  10.3 0.0 collective-permute-done.4.refs_8_
  10.3 1.6 %shard_map.48 = (f32[128,1024]{1,0:T(8,128)S(1)}, f32[16,1024]{1,0:T(8,128)S(1)}, f32[128,1024]{1,0:T(8,128)S(1)}, f32[16,1024]{1,0:T(8,128)S(1)}) custom-call(f32[8,512]{1,0:T(8,128)S(1)} %flags.1.refs_0_, f32[128,1024]{1,0:T(8,128)S(1)} %get-tuple-element.55.refs_1_, f32[16,1024]{1,0:T(8,128)S(1)} %get-tuple-element.56.refs_2_, ...), custom_call_target="tpu_custom_call" | custom-call | flops 536870912 | bytes 2097152 | tf_op jit(solution)/shard_map/pallas_call | solution.py:255
  11.9 0.8 %collective-permute-done.3.refs_6_ = bf16[2,256,128]{2,1,0:T(8,128)(2,1)S(1)} collective-permute-done((bf16[2,256,128]{2,1,0:T(8,128)(2,1)S(1)}, bf16[2,256,128]{2,1,0:T(8,128)(2,1)S(1)}, u32[]{:S(2)}, u32[]{:S(2)}) %collective-permute-start.3) | collective-permute-done | bytes 131104 | tf_op jit(solution)/shard_map/ppermute | solution.py:291
  12.7 0.9 %collective-permute-start.5 = (bf16[2,256,128]{2,1,0:T(8,128)(2,1)S(1)}, bf16[2,256,128]{2,1,0:T(8,128)(2,1)S(1)}, u32[]{:S(2)}, u32[]{:S(2)}) collective-permute-start(bf16[2,256,128]{2,1,0:T(8,128)(2,1)S(1)} %collective-permute-done.3.refs_6_), channel_id=1, source_target_pairs={{0,1},{1,0},{2,3},{3,2},{4,5},{5,4},{6,7},{7,6},{8,9},{9,8},{10,11... | collective-permute-start | bytes 393224 | tf_op jit(solution)/shard_map/ppermute | solution.py:286
  13.5 1.3 %collective-permute-start.2 = (bf16[2,256,128]{2,1,0:T(8,128)(2,1)S(1)}, bf16[2,256,128]{2,1,0:T(8,128)(2,1)S(1)}, u32[]{:S(2)}, u32[]{:S(2)}) collective-permute-start(bf16[2,256,128]{2,1,0:T(8,128)(2,1)S(1)} %collective-permute-done.refs_7_), channel_id=1, source_target_pairs={{0,1},{1,0},{4,8},{5,9},{8,12},{9,13},{12,4},{13,5},{2,3},{3,2},{6... | collective-permute-start | bytes 393224 | tf_op jit(solution)/shard_map/ppermute | solution.py:336
  14.8 0.1 shard_map.49
  14.9 0.0 collective-permute-done.5.refs_6_
  14.9 0.1 shard_map.50
  15.1 6.5 %collective-permute-done.2.refs_6_ = bf16[2,256,128]{2,1,0:T(8,128)(2,1)S(1)} collective-permute-done((bf16[2,256,128]{2,1,0:T(8,128)(2,1)S(1)}, bf16[2,256,128]{2,1,0:T(8,128)(2,1)S(1)}, u32[]{:S(2)}, u32[]{:S(2)}) %collective-permute-start.2) | collective-permute-done | bytes 131104 | tf_op jit(solution)/shard_map/ppermute | solution.py:336
  21.5 0.6 %collective-permute-start.6 = (bf16[2,256,128]{2,1,0:T(8,128)(2,1)S(1)}, bf16[2,256,128]{2,1,0:T(8,128)(2,1)S(1)}, u32[]{:S(2)}, u32[]{:S(2)}) collective-permute-start(bf16[2,256,128]{2,1,0:T(8,128)(2,1)S(1)} %collective-permute-done.2.refs_6_), channel_id=1, source_target_pairs={{0,1},{1,0},{2,3},{3,2},{4,5},{5,4},{6,7},{7,6},{8,9},{9,8},{10,11... | collective-permute-start | bytes 393224 | tf_op jit(solution)/shard_map/ppermute | solution.py:286
  22.1 0.1 shard_map.51
  22.2 0.9 %collective-permute-done.6.refs_6_ = bf16[2,256,128]{2,1,0:T(8,128)(2,1)S(1)} collective-permute-done((bf16[2,256,128]{2,1,0:T(8,128)(2,1)S(1)}, bf16[2,256,128]{2,1,0:T(8,128)(2,1)S(1)}, u32[]{:S(2)}, u32[]{:S(2)}) %collective-permute-start.6) | collective-permute-done | bytes 131104 | tf_op jit(solution)/shard_map/ppermute | solution.py:286
  23.1 0.9 %shard_map.52 = bf16[2048,128]{1,0:T(8,128)(2,1)} custom-call(f32[128,1024]{1,0:T(8,128)S(1)} %get-tuple-element.87.refs_0_, f32[16,1024]{1,0:T(8,128)S(1)} %get-tuple-element.88.refs_1_, bf16[1024,256]{1,0:T(8,128)(2,1)S(1)} %get-tuple-element.82.refs_3_.refs_2_, f32[128,1024]{1,0:T(8,128)S(1)} %get-tuple-element.89.refs_3_, ...), custom_call_target="tpu_custom_call" | custom-call | flops 268435456 | bytes 2097152 | tf_op jit(solution)/shard_map/pallas_call | solution.py:255
  (4 shorter events, 0.0 us)
Async XLA Ops:
  0.0 3.0 %copy-start = (bf16[512,1,4,128]{3,2,1,0:T(4,128)(2,1)S(1)}, bf16[512,1,4,128]{3,2,1,0:T(4,128)(2,1)}, u32[]{:S(2)}) copy-start(bf16[512,1,4,128]{3,2,1,0:T(4,128)(2,1)} %param.4) | copy-start | bytes 1572868
  1.0 2.0 %collective-permute-start.1 = (bf16[2,256,128]{2,1,0:T(8,128)(2,1)S(1)}, bf16[2,256,128]{2,1,0:T(8,128)(2,1)S(1)}, u32[]{:S(2)}, u32[]{:S(2)}) collective-permute-start(bf16[2,256,128]{2,1,0:T(8,128)(2,1)S(1)} %pad_maximum_fusion.refs_0_), channel_id=1, source_target_pairs={{0,1},{1,0},{2,3},{3,2},{4,5},{5,4},{6,7},{7,6},{8,9},{9,8},{10,11... | collective-permute-start | bytes 393224 | tf_op jit(solution)/shard_map/ppermute | solution.py:286
  1.7 5.0 %collective-permute-start = (bf16[2,256,128]{2,1,0:T(8,128)(2,1)S(1)}, bf16[2,256,128]{2,1,0:T(8,128)(2,1)S(1)}, u32[]{:S(2)}, u32[]{:S(2)}) collective-permute-start(bf16[2,256,128]{2,1,0:T(8,128)(2,1)S(1)} %pad_maximum_fusion.refs_0_), channel_id=1, source_target_pairs={{0,4},{4,8},{8,12},{12,0},{1,5},{5,9},{9,13},{13,1},{2,6},{6,10},{... | collective-permute-start | bytes 393224 | tf_op jit(solution)/shard_map/ppermute | solution.py:291
  6.7 3.0 %copy-start.1 = (s32[2,7]{1,0:T(2,128)S(1)}, s32[2,7]{1,0:T(2,128)}, u32[]{:S(2)}) copy-start(s32[2,7]{1,0:T(2,128)} %table_ref.1) | copy-start | bytes 172
  6.7 3.6 %collective-permute-start.4 = (bf16[2,256,128]{2,1,0:T(8,128)(2,1)S(1)}, bf16[2,256,128]{2,1,0:T(8,128)(2,1)S(1)}, u32[]{:S(2)}, u32[]{:S(2)}) collective-permute-start(bf16[2,256,128]{2,1,0:T(8,128)(2,1)S(1)} %collective-permute-done.refs_7_), channel_id=1, source_target_pairs={{0,1},{1,0},{2,3},{3,2},{4,5},{5,4},{6,7},{7,6},{8,9},{9,8},{10,11... | collective-permute-start | bytes 393224 | tf_op jit(solution)/shard_map/ppermute | solution.py:286
  7.6 5.1 %collective-permute-start.3 = (bf16[2,256,128]{2,1,0:T(8,128)(2,1)S(1)}, bf16[2,256,128]{2,1,0:T(8,128)(2,1)S(1)}, u32[]{:S(2)}, u32[]{:S(2)}) collective-permute-start(bf16[2,256,128]{2,1,0:T(8,128)(2,1)S(1)} %pad_maximum_fusion.refs_0_), channel_id=1, source_target_pairs={{0,12},{4,0},{8,4},{12,8},{1,13},{5,1},{9,5},{13,9},{2,14},{6,2},{... | collective-permute-start | bytes 393224 | tf_op jit(solution)/shard_map/ppermute | solution.py:291
  12.7 2.2 %collective-permute-start.5 = (bf16[2,256,128]{2,1,0:T(8,128)(2,1)S(1)}, bf16[2,256,128]{2,1,0:T(8,128)(2,1)S(1)}, u32[]{:S(2)}, u32[]{:S(2)}) collective-permute-start(bf16[2,256,128]{2,1,0:T(8,128)(2,1)S(1)} %collective-permute-done.3.refs_6_), channel_id=1, source_target_pairs={{0,1},{1,0},{2,3},{3,2},{4,5},{5,4},{6,7},{7,6},{8,9},{9,8},{10,11... | collective-permute-start | bytes 393224 | tf_op jit(solution)/shard_map/ppermute | solution.py:286
  13.5 8.0 %collective-permute-start.2 = (bf16[2,256,128]{2,1,0:T(8,128)(2,1)S(1)}, bf16[2,256,128]{2,1,0:T(8,128)(2,1)S(1)}, u32[]{:S(2)}, u32[]{:S(2)}) collective-permute-start(bf16[2,256,128]{2,1,0:T(8,128)(2,1)S(1)} %collective-permute-done.refs_7_), channel_id=1, source_target_pairs={{0,1},{1,0},{4,8},{5,9},{8,12},{9,13},{12,4},{13,5},{2,3},{3,2},{6... | collective-permute-start | bytes 393224 | tf_op jit(solution)/shard_map/ppermute | solution.py:336
  21.5 1.6 %collective-permute-start.6 = (bf16[2,256,128]{2,1,0:T(8,128)(2,1)S(1)}, bf16[2,256,128]{2,1,0:T(8,128)(2,1)S(1)}, u32[]{:S(2)}, u32[]{:S(2)}) collective-permute-start(bf16[2,256,128]{2,1,0:T(8,128)(2,1)S(1)} %collective-permute-done.2.refs_6_), channel_id=1, source_target_pairs={{0,1},{1,0},{2,3},{3,2},{4,5},{5,4},{6,7},{7,6},{8,9},{9,8},{10,11... | collective-permute-start | bytes 393224 | tf_op jit(solution)/shard_map/ppermute | solution.py:286
where the time goes:
time: 24.2 us; the launch traced here: 24 us
  waiting for transfers between devices  9.81 us (41%)
  starting transfers between devices  7.72 us (32%)
  Pallas kernels  5.43 us (22%)
  local copies, waits for them, and re-layouts  0.95 us (4%)
    ppermute x1, waiting for transfers between devices, shards(): two = lax.ppermute(one, ('ctx', 'qsub'), route)  6.46 us
    ppermute x2, starting transfers between devices, hop(): return lax.ppermute(block, 'ctx', route)  3.32 us
    ppermute x4, starting transfers between devices, swapped(): lax.ppermute(arrived, 'qsub', [(c, (c + shift) % cores) for c in range(co...  3.1 us
    pallas_call x5, Pallas kernels, call_arrival(): pl.pallas_call(functools.partial(arrival_stage, source, row_of, len(array...  2.84 us
    ppermute x2, waiting for transfers between devices, hop(): return lax.ppermute(block, 'ctx', route)  2.46 us
    pallas_call x2, Pallas kernels, call_local(): pl.pallas_call(functools.partial(local_stage, i, per_head, len(parts)), i...  1.99 us
    ppermute x1, starting transfers between devices, shards(): two = lax.ppermute(one, ('ctx', 'qsub'), route)  1.3 us
    another operation x1, local copies, waits for them, and re-layouts, shards(): jnp.stack([lax.dynamic_slice_in_dim(k, core * part, part), lax.dynamic_sl...  0.94 us
  transfers between devices with their start and end apart: 7, of which 4 were waited for; matrix products, arithmetic and copies ran while one was open for 0% of the time, Pallas kernels for 19%

commit v1 on v0

--- a/solution.py
+++ b/solution.py
@@ -115,16 +115,21 @@
                     at += 1
 
 
-def arrival_stage(source, row_of, operands, blocks_here, last, *refs):
+def arrival_stage(source, row_of, operands, blocks_here, last, early, *refs):
     refs = list(refs)
     flags_ref = None if row_of is None else refs.pop(0)
     state_in = [(refs.pop(0), refs.pop(0), refs.pop(0)) for _ in range(blocks_here)]
     arrived = [refs.pop(0) for _ in range(operands)]
     if last:
+        if early:
+            refs.pop(0)
         out_hbm, out_ref, k_ref, vt_ref, sems = refs
     else:
         state_out = [(refs.pop(0), refs.pop(0)) for _ in range(blocks_here)]
-        k_ref, vt_ref = refs
+        if early:
+            out_hbm, out_ref, k_ref, vt_ref, sems = refs
+        else:
+            k_ref, vt_ref = refs
     me = lax.axis_index("ctx")
     origin = source(me)
     some = (origin >= 0) & (origin < me)
@@ -143,6 +148,9 @@
         if not last:
             keep_state(*state_out[i], cols, acc, highest, total)
             return
+        write(t, acc, total)
+
+    def write(t, acc, total):
         rows = pl.ds(t * tile, tile)
         out_ref[rows, :] = (acc * (1.0 / total[:1])).astype(out_ref.dtype).T
         pltpu.make_async_copy(out_ref.at[rows], out_hbm.at[rows], sems.at[t]).start()
@@ -184,17 +192,29 @@
             keep = jnp.exp2(before - highest)
             finish(t, acc_in[:, cols] * keep + sums[:DH], highest, stat_in[8:, cols] * keep + sums[DH : DH + 8])
 
+    def arrive():
+        for t in range(tiles):
+            rows = pl.ds(t * tile, tile)
+            pltpu.make_async_copy(out_ref.at[rows], out_hbm.at[rows], sems.at[t]).wait()
+
+    if last and early:
+        pl.when(some)(arrive)
+        return
+
     @pl.when(jnp.logical_not(some))
     def _():
         for t in range(tiles):
             i, cols = place(t)
             acc_in, stat_in, _ = state_in[i]
-            finish(t, acc_in[:, cols], stat_in[:1, cols], stat_in[8:, cols])
+            if early:
+                write(t, acc_in[:, cols], stat_in[8:, cols])
+            else:
+                finish(t, acc_in[:, cols], stat_in[:1, cols], stat_in[8:, cols])
+        if early:
+            arrive()
 
     if last:
-        for t in range(tiles):
-            rows = pl.ds(t * tile, tile)
-            pltpu.make_async_copy(out_ref.at[rows], out_hbm.at[rows], sems.at[t]).wait()
+        arrive()
 
 
 VMEM_SPEC = pl.BlockSpec(memory_space=pltpu.VMEM)
@@ -242,26 +262,42 @@
     )(table)
 
 
-def call_arrival(source, row_of, arrays, flags, state, last=False):
+def call_arrival(source, row_of, arrays, flags, state, last=False, early=False, written=None):
     rows_per_block = state[0][0].shape[1]
     rows = rows_per_block * len(state)
     dtype = arrays[0].dtype
     keys = sum(a.shape[1] for a in arrays)
     scratch = [pltpu.VMEM((keys, 2 * DH), dtype), pltpu.VMEM((DH + ONES, keys), dtype)]
-    if last:
+    early = early or written is not None
+    if last or early:
         scratch = [pltpu.VMEM((rows, DH), dtype), *scratch, pltpu.SemaphoreType.DMA((rows // min(TILE, keys),))]
     args = [] if row_of is None else [flags]
     args += [*[a for block in state for a in block], *arrays]
+    in_specs = [VMEM_SPEC] * len(args)
+    output = jax.ShapeDtypeStruct((rows, DH), dtype)
+    out_shape, out_specs = [], []
+    if not last:
+        out_shape, out_specs = state_shapes(rows_per_block) * len(state), [VMEM_SPEC] * (2 * len(state))
+    if last or early:
+        out_shape, out_specs = [*out_shape, output], [*out_specs, ANY_SPEC]
+    aliases = {}
+    if written is not None:
+        aliases = {len(args): 0}
+        args, in_specs = [*args, written], [*in_specs, ANY_SPEC]
     out = pl.pallas_call(
-        functools.partial(arrival_stage, source, row_of, len(arrays), len(state), last),
-        in_specs=[VMEM_SPEC] * len(args),
-        out_specs=ANY_SPEC if last else [VMEM_SPEC] * (2 * len(state)),
-        out_shape=jax.ShapeDtypeStruct((rows, DH), dtype) if last else state_shapes(rows_per_block) * len(state),
+        functools.partial(arrival_stage, source, row_of, len(arrays), len(state), last, early),
+        in_specs=in_specs,
+        out_specs=out_specs,
+        out_shape=out_shape,
         scratch_shapes=scratch,
+        input_output_aliases=aliases,
         cost_estimate=cost(rows, keys),
         compiler_params=PARAMS,
     )(*args)
-    return out if last else [(out[2 * i], out[2 * i + 1], block[2]) for i, block in enumerate(state)]
+    if last:
+        return out[0]
+    state = [(out[2 * i], out[2 * i + 1], block[2]) for i, block in enumerate(state)]
+    return (state, out[-1]) if early else state
 
 
 def shards(queries, key_states, value_states, block_table):
@@ -339,9 +375,12 @@
             arrived, state = lax.optimization_barrier((arrived, state))
             swap = swapped(arrived)
             row = row_of[n]
-            state = call_arrival(sources[n], row, [arrived], flags, state)
+            written = None
+            state = call_arrival(sources[n], row, [arrived], flags, state, early=n == 2)
+            if n == 2:
+                state, written = state
             row = None if row is None else row + per_core * blocks_here
-            state = call_arrival(sources[n], row, swap, flags, state, last=n == 2)
+            state = call_arrival(sources[n], row, swap, flags, state, last=n == 2, written=written)
         attended = state
     else:
         parts = [packed, *swapped(packed)]

time: 24.2 us -> 24.2 us (level)
  the two profiles are of different devices: /device:TPU:9 before, /device:TPU:25 now
where the time goes in v1:
time: 24.2 us; the launch traced here: 24 us
  waiting for transfers between devices  10.6 us (44%)
  Pallas kernels  8.86 us (37%)
  starting transfers between devices  3.56 us (15%)
  local copies, waits for them, and re-layouts  0.95 us (4%)
    pallas_call x5, Pallas kernels, call_arrival(): pl.pallas_call(functools.partial(arrival_stage, source, row_of, len(array...  6.28 us
    ppermute x2, waiting for transfers between devices, hop(): return lax.ppermute(block, 'ctx', route)  6.25 us
    ppermute x4, starting transfers between devices, swapped(): lax.ppermute(arrived, 'qsub', [(c, (c + shift) % cores) for c in range(co...  3.38 us
    ppermute x1, waiting for transfers between devices, shards(): two = lax.ppermute(one, ('ctx', 'qsub'), route)  3.11 us
    pallas_call x2, Pallas kernels, call_local(): pl.pallas_call(functools.partial(local_stage, i, per_head, len(parts)), i...  1.99 us
    ppermute x4, waiting for transfers between devices, swapped(): lax.ppermute(arrived, 'qsub', [(c, (c + shift) % cores) for c in range(co...  1.22 us
    another operation x1, local copies, waits for them, and re-layouts, shards(): jnp.stack([lax.dynamic_slice_in_dim(k, core * part, part), lax.dynamic_sl...  0.94 us
    pallas_call x1, Pallas kernels, call_flags(): pl.pallas_call(functools.partial(flags_stage, stages, blocks_here), in_sp...  0.6 us
  transfers between devices with their start and end apart: 7, of which 5 were waited for; matrix products, arithmetic and copies ran while one was open for 0% of the time, Pallas kernels for 30%

profile of v1, /device:TPU:25, one launch (start us, length us, event | category | flops | bytes accessed | tf_op | source)
XLA Modules:
  0.0 24.0 jit_solution(632229128871238715)
XLA Ops:
  0.0 0.9 %dynamic-slice_bitcast_fusion = (bf16[1,256,128]{2,1,0:T(8,128)(2,1)S(1)}, bf16[1,256,128]{2,1,0:T(8,128)(2,1)S(1)}) fusion(bf16[512,1,128]{2,0,1:T(8,128)(2,1)} %param.6, s32[]{:T(128)S(6)} %select_n.4, bf16[512,1,128]{2,0,1:T(8,128)(2,1)} %param.5), kind=kLoop, calls=%fused_computation.1 | loop fusion | bytes 262148 | tf_op jit(solution)/shard_map/stack | solution.py:316
  1.0 0.7 %collective-permute-start.1 = (bf16[2,256,128]{2,1,0:T(8,128)(2,1)S(1)}, bf16[2,256,128]{2,1,0:T(8,128)(2,1)S(1)}, u32[]{:S(2)}, u32[]{:S(2)}) collective-permute-start(bf16[2,256,128]{2,1,0:T(8,128)(2,1)S(1)} %pad_maximum_fusion.refs_0_), channel_id=1, source_target_pairs={{0,1},{1,0},{2,3},{3,2},{4,5},{5,4},{6,7},{7,6},{8,9},{9,8},{10,11... | collective-permute-start | bytes 393224 | tf_op jit(solution)/shard_map/ppermute | solution.py:322
  1.7 0.0 collective-permute-start
  1.7 1.0 %collective-permute-done.1.refs_1_ = bf16[2,256,128]{2,1,0:T(8,128)(2,1)S(1)} collective-permute-done((bf16[2,256,128]{2,1,0:T(8,128)(2,1)S(1)}, bf16[2,256,128]{2,1,0:T(8,128)(2,1)S(1)}, u32[]{:S(2)}, u32[]{:S(2)}) %collective-permute-start.1) | collective-permute-done | bytes 131104 | tf_op jit(solution)/shard_map/ppermute | solution.py:322
  2.7 0.0 copy-done
  2.7 0.8 %shard_map.46 = (f32[128,1024]{1,0:T(8,128)S(1)}, f32[16,1024]{1,0:T(8,128)S(1)}, bf16[1024,256]{1,0:T(8,128)(2,1)S(1)}) custom-call(bf16[2048,128]{1,0:T(8,128)(2,1)S(1)} %bitcast.8, bf16[2,256,128]{2,1,0:T(8,128)(2,1)S(1)} %pad_maximum_fusion.refs_0_, bf16[2,256,128]{2,1,0:T(8,128)(2,1)S(1)} %collective-permute-done.1.refs_1_), custom_call_target="tpu_custom_call" | custom-call | flops 134217728 | bytes 1048576 | tf_op jit(solution)/shard_map/pallas_call | solution.py:238
  3.5 1.2 %shard_map.47 = (f32[128,1024]{1,0:T(8,128)S(1)}, f32[16,1024]{1,0:T(8,128)S(1)}, bf16[1024,256]{1,0:T(8,128)(2,1)S(1)}) custom-call(bf16[2048,128]{1,0:T(8,128)(2,1)S(1)} %bitcast.9, bf16[2,256,128]{2,1,0:T(8,128)(2,1)S(1)} %pad_maximum_fusion.refs_0_, bf16[2,256,128]{2,1,0:T(8,128)(2,1)S(1)} %collective-permute-done.1.refs_1_), custom_call_target="tpu_custom_call" | custom-call | flops 268435456 | bytes 1048576 | tf_op jit(solution)/shard_map/pallas_call | solution.py:238
  4.7 2.0 %collective-permute-done.refs_7_ = bf16[2,256,128]{2,1,0:T(8,128)(2,1)S(1)} collective-permute-done((bf16[2,256,128]{2,1,0:T(8,128)(2,1)S(1)}, bf16[2,256,128]{2,1,0:T(8,128)(2,1)S(1)}, u32[]{:S(2)}, u32[]{:S(2)}) %collective-permute-start) | collective-permute-done | bytes 131104 | tf_op jit(solution)/shard_map/ppermute | solution.py:327
  6.7 0.9 %collective-permute-start.4 = (bf16[2,256,128]{2,1,0:T(8,128)(2,1)S(1)}, bf16[2,256,128]{2,1,0:T(8,128)(2,1)S(1)}, u32[]{:S(2)}, u32[]{:S(2)}) collective-permute-start(bf16[2,256,128]{2,1,0:T(8,128)(2,1)S(1)} %collective-permute-done.refs_7_), channel_id=1, source_target_pairs={{0,1},{1,0},{2,3},{3,2},{4,5},{5,4},{6,7},{7,6},{8,9},{9,8},{10,11... | collective-permute-start | bytes 393224 | tf_op jit(solution)/shard_map/ppermute | solution.py:322
  7.6 0.2 collective-permute-start.3
  7.8 0.6 %flags.1.refs_0_ = f32[8,512]{1,0:T(8,128)S(1)} custom-call(s32[2,7]{1,0:T(2,128)S(1)} %copy-done.1), custom_call_target="tpu_custom_call" | custom-call | tf_op jit(solution)/shard_map/flags/pallas_call | solution.py:255
  8.4 0.2 collective-permute-done.4.refs_8_
  8.6 1.6 %shard_map.48 = (f32[128,1024]{1,0:T(8,128)S(1)}, f32[16,1024]{1,0:T(8,128)S(1)}, f32[128,1024]{1,0:T(8,128)S(1)}, f32[16,1024]{1,0:T(8,128)S(1)}) custom-call(f32[8,512]{1,0:T(8,128)S(1)} %flags.1.refs_0_, f32[128,1024]{1,0:T(8,128)S(1)} %get-tuple-element.56.refs_1_, f32[16,1024]{1,0:T(8,128)S(1)} %get-tuple-element.57.refs_2_, ...), custom_call_target="tpu_custom_call" | custom-call | flops 536870912 | bytes 2097152 | tf_op jit(solution)/shard_map/pallas_call | solution.py:287
  10.2 4.2 %collective-permute-done.3.refs_6_ = bf16[2,256,128]{2,1,0:T(8,128)(2,1)S(1)} collective-permute-done((bf16[2,256,128]{2,1,0:T(8,128)(2,1)S(1)}, bf16[2,256,128]{2,1,0:T(8,128)(2,1)S(1)}, u32[]{:S(2)}, u32[]{:S(2)}) %collective-permute-start.3) | collective-permute-done | bytes 131104 | tf_op jit(solution)/shard_map/ppermute | solution.py:327
  14.5 0.9 %collective-permute-start.5 = (bf16[2,256,128]{2,1,0:T(8,128)(2,1)S(1)}, bf16[2,256,128]{2,1,0:T(8,128)(2,1)S(1)}, u32[]{:S(2)}, u32[]{:S(2)}) collective-permute-start(bf16[2,256,128]{2,1,0:T(8,128)(2,1)S(1)} %collective-permute-done.3.refs_6_), channel_id=1, source_target_pairs={{0,1},{1,0},{2,3},{3,2},{4,5},{5,4},{6,7},{7,6},{8,9},{9,8},{10,11... | collective-permute-start | bytes 393224 | tf_op jit(solution)/shard_map/ppermute | solution.py:322
  15.3 0.0 collective-permute-start.2
  15.3 0.9 %shard_map.49 = (f32[128,1024]{1,0:T(8,128)S(1)}, f32[16,1024]{1,0:T(8,128)S(1)}, f32[128,1024]{1,0:T(8,128)S(1)}, f32[16,1024]{1,0:T(8,128)S(1)}) custom-call(f32[128,1024]{1,0:T(8,128)S(1)} %get-tuple-element.66.refs_0_, f32[16,1024]{1,0:T(8,128)S(1)} %get-tuple-element.67.refs_1_, bf16[1024,256]{1,0:T(8,128)(2,1)S(1)} %get-tuple-element.83.refs_3_.refs_2_, ...), custom_call_target="tpu_custom_call" | custom-call | flops 268435456 | bytes 2097152 | tf_op jit(solution)/shard_map/pallas_call | solution.py:287
  16.3 0.0 collective-permute-done.5.refs_6_
  16.3 0.9 %shard_map.50 = (f32[128,1024]{1,0:T(8,128)S(1)}, f32[16,1024]{1,0:T(8,128)S(1)}, f32[128,1024]{1,0:T(8,128)S(1)}, f32[16,1024]{1,0:T(8,128)S(1)}) custom-call(f32[128,1024]{1,0:T(8,128)S(1)} %get-tuple-element.73.refs_0_, f32[16,1024]{1,0:T(8,128)S(1)} %get-tuple-element.74.refs_1_, bf16[1024,256]{1,0:T(8,128)(2,1)S(1)} %get-tuple-element.83.refs_3_.refs_2_, ...), custom_call_target="tpu_custom_call" | custom-call | flops 268435456 | bytes 2097152 | tf_op jit(solution)/shard_map/pallas_call | solution.py:287
  17.3 3.1 %collective-permute-done.2.refs_6_ = bf16[2,256,128]{2,1,0:T(8,128)(2,1)S(1)} collective-permute-done((bf16[2,256,128]{2,1,0:T(8,128)(2,1)S(1)}, bf16[2,256,128]{2,1,0:T(8,128)(2,1)S(1)}, u32[]{:S(2)}, u32[]{:S(2)}) %collective-permute-start.2) | collective-permute-done | bytes 131104 | tf_op jit(solution)/shard_map/ppermute | solution.py:372
  20.4 0.9 %collective-permute-start.6 = (bf16[2,256,128]{2,1,0:T(8,128)(2,1)S(1)}, bf16[2,256,128]{2,1,0:T(8,128)(2,1)S(1)}, u32[]{:S(2)}, u32[]{:S(2)}) collective-permute-start(bf16[2,256,128]{2,1,0:T(8,128)(2,1)S(1)} %collective-permute-done.2.refs_6_), channel_id=1, source_target_pairs={{0,1},{1,0},{2,3},{3,2},{4,5},{5,4},{6,7},{7,6},{8,9},{9,8},{10,11... | collective-permute-start | bytes 393224 | tf_op jit(solution)/shard_map/ppermute | solution.py:322
  21.2 1.0 %shard_map.51 = (f32[128,1024]{1,0:T(8,128)S(1)}, f32[16,1024]{1,0:T(8,128)S(1)}, f32[128,1024]{1,0:T(8,128)S(1)}, f32[16,1024]{1,0:T(8,128)S(1)}, bf16[2048,128]{1,0:T(8,128)(2,1)}) custom-call(f32[128,1024]{1,0:T(8,128)S(1)} %get-tuple-element.81.refs_0_, f32[16,1024]{1,0:T(8,128)S(1)} %get-tuple-element.82.refs_1_, ...), custom_call_target="tpu_custom_call" | custom-call | flops 268435456 | bytes 2097152 | tf_op jit(solution)/shard_map/pallas_call | solution.py:287
  22.3 0.0 collective-permute-done.6.refs_6_
  22.3 1.7 %shard_map.52 = bf16[2048,128]{1,0:T(8,128)(2,1)} custom-call(f32[128,1024]{1,0:T(8,128)S(1)} %get-tuple-element.88.refs_0_, f32[16,1024]{1,0:T(8,128)S(1)} %get-tuple-element.89.refs_1_, bf16[1024,256]{1,0:T(8,128)(2,1)S(1)} %get-tuple-element.83.refs_3_.refs_2_, f32[128,1024]{1,0:T(8,128)S(1)} %get-tuple-element.90.refs_3_, ...), custom_call_target="tpu_custom_call", output_to_operand_aliasing={{}: (7, {})} | custom-call | flops 268435456 | bytes 2097152 | tf_op jit(solution)/shard_map/pallas_call | solution.py:287
  (4 shorter events, 0.0 us)
Async XLA Ops:
  0.0 2.7 %copy-start = (bf16[512,1,4,128]{3,2,1,0:T(4,128)(2,1)S(1)}, bf16[512,1,4,128]{3,2,1,0:T(4,128)(2,1)}, u32[]{:S(2)}) copy-start(bf16[512,1,4,128]{3,2,1,0:T(4,128)(2,1)} %param.4) | copy-start | bytes 1572868
  1.0 1.7 %collective-permute-start.1 = (bf16[2,256,128]{2,1,0:T(8,128)(2,1)S(1)}, bf16[2,256,128]{2,1,0:T(8,128)(2,1)S(1)}, u32[]{:S(2)}, u32[]{:S(2)}) collective-permute-start(bf16[2,256,128]{2,1,0:T(8,128)(2,1)S(1)} %pad_maximum_fusion.refs_0_), channel_id=1, source_target_pairs={{0,1},{1,0},{2,3},{3,2},{4,5},{5,4},{6,7},{7,6},{8,9},{9,8},{10,11... | collective-permute-start | bytes 393224 | tf_op jit(solution)/shard_map/ppermute | solution.py:322
  1.7 5.0 %collective-permute-start = (bf16[2,256,128]{2,1,0:T(8,128)(2,1)S(1)}, bf16[2,256,128]{2,1,0:T(8,128)(2,1)S(1)}, u32[]{:S(2)}, u32[]{:S(2)}) collective-permute-start(bf16[2,256,128]{2,1,0:T(8,128)(2,1)S(1)} %pad_maximum_fusion.refs_0_), channel_id=1, source_target_pairs={{0,4},{4,8},{8,12},{12,0},{1,5},{5,9},{9,13},{13,1},{2,6},{6,10},{... | collective-permute-start | bytes 393224 | tf_op jit(solution)/shard_map/ppermute | solution.py:327
  6.7 1.1 %copy-start.1 = (s32[2,7]{1,0:T(2,128)S(1)}, s32[2,7]{1,0:T(2,128)}, u32[]{:S(2)}) copy-start(s32[2,7]{1,0:T(2,128)} %table_ref.1) | copy-start | bytes 172
  6.7 1.9 %collective-permute-start.4 = (bf16[2,256,128]{2,1,0:T(8,128)(2,1)S(1)}, bf16[2,256,128]{2,1,0:T(8,128)(2,1)S(1)}, u32[]{:S(2)}, u32[]{:S(2)}) collective-permute-start(bf16[2,256,128]{2,1,0:T(8,128)(2,1)S(1)} %collective-permute-done.refs_7_), channel_id=1, source_target_pairs={{0,1},{1,0},{2,3},{3,2},{4,5},{5,4},{6,7},{7,6},{8,9},{9,8},{10,11... | collective-permute-start | bytes 393224 | tf_op jit(solution)/shard_map/ppermute | solution.py:322
  7.6 6.8 %collective-permute-start.3 = (bf16[2,256,128]{2,1,0:T(8,128)(2,1)S(1)}, bf16[2,256,128]{2,1,0:T(8,128)(2,1)S(1)}, u32[]{:S(2)}, u32[]{:S(2)}) collective-permute-start(bf16[2,256,128]{2,1,0:T(8,128)(2,1)S(1)} %pad_maximum_fusion.refs_0_), channel_id=1, source_target_pairs={{0,12},{4,0},{8,4},{12,8},{1,13},{5,1},{9,5},{13,9},{2,14},{6,2},{... | collective-permute-start | bytes 393224 | tf_op jit(solution)/shard_map/ppermute | solution.py:327
  14.5 1.8 %collective-permute-start.5 = (bf16[2,256,128]{2,1,0:T(8,128)(2,1)S(1)}, bf16[2,256,128]{2,1,0:T(8,128)(2,1)S(1)}, u32[]{:S(2)}, u32[]{:S(2)}) collective-permute-start(bf16[2,256,128]{2,1,0:T(8,128)(2,1)S(1)} %collective-permute-done.3.refs_6_), channel_id=1, source_target_pairs={{0,1},{1,0},{2,3},{3,2},{4,5},{5,4},{6,7},{7,6},{8,9},{9,8},{10,11... | collective-permute-start | bytes 393224 | tf_op jit(solution)/shard_map/ppermute | solution.py:322
  15.3 5.1 %collective-permute-start.2 = (bf16[2,256,128]{2,1,0:T(8,128)(2,1)S(1)}, bf16[2,256,128]{2,1,0:T(8,128)(2,1)S(1)}, u32[]{:S(2)}, u32[]{:S(2)}) collective-permute-start(bf16[2,256,128]{2,1,0:T(8,128)(2,1)S(1)} %collective-permute-done.refs_7_), channel_id=1, source_target_pairs={{0,1},{1,0},{4,8},{5,9},{8,12},{9,13},{12,4},{13,5},{2,3},{3,2},{6... | collective-permute-start | bytes 393224 | tf_op jit(solution)/shard_map/ppermute | solution.py:372
  20.4 1.9 %collective-permute-start.6 = (bf16[2,256,128]{2,1,0:T(8,128)(2,1)S(1)}, bf16[2,256,128]{2,1,0:T(8,128)(2,1)S(1)}, u32[]{:S(2)}, u32[]{:S(2)}) collective-permute-start(bf16[2,256,128]{2,1,0:T(8,128)(2,1)S(1)} %collective-permute-done.2.refs_6_), channel_id=1, source_target_pairs={{0,1},{1,0},{2,3},{3,2},{4,5},{5,4},{6,7},{7,6},{8,9},{9,8},{10,11... | collective-permute-start | bytes 393224 | tf_op jit(solution)/shard_map/ppermute | solution.py:322
